TPU v7x, 128 devices: a whole 4x4x4 slice. The times are simulated.
128 devices in a mesh: cluster: 8 (over x, core), row: 16 (over z, y).
Axes of the slice: x: 4, y: 4, z: 4, core: 2. Of those that a mesh axis runs over, the one named last changes fastest.
Arguments:
- sources: bfloat16 [32768, 512], P(('cluster', 'row')), may hold values from -12 to 12
- targets: bfloat16 [32768, 512], P(('cluster', 'row')), may hold values from -12 to 12
- source_order: int32 [32768], P(('cluster', 'row')), may hold values from 0 to 255, as said below
- target_order: int32 [32768], P(('cluster', 'row')), may hold values from 0 to 255, as said below
Outputs:
- source_map: bfloat16 [32768, 512], P(('cluster', 'row'))
- target_map: bfloat16 [32768, 512], P(('cluster', 'row'))
Inputs may be any that keep to these rules, and one draw needn't show every extreme that they name: `source_order`: in each aligned block of 256 consecutive rows every value appears exactly once, so each block holds 32 source rows of every co-cluster. `target_order`: in each aligned block of 256 consecutive rows every value appears exactly once, so each block holds 32 target rows of every co-cluster.
All inputs are finite; a program needn't handle non-finite values.
Results may differ from a plain program's by a relative error of at most 0.01.
Values may be sent and summed in bfloat16 or wider, within the bound.
No kernel may reach another device: no remote copies, remote signals or barrier semaphores. Data moves between devices by JAX's collectives and lax.ppermute only.
A program may use at most 64 MiB of HBM per device.

v0:
```python
import math
import jax
import jax.numpy as jnp
from jax import lax
from jax.sharding import PartitionSpec as P

ITERS = 3
entropy_weight = 0.02


def square_sums(matrix):
    widened = matrix.astype(jnp.float32)
    return jnp.sum(widened * widened, axis=1)


def cost_panel(source_rows, source_norms, target_rows, target_norms):
    inner = jnp.einsum("id,jd->ij", source_rows, target_rows, preferred_element_type=jnp.float32)
    return (source_norms[:, None] + target_norms[None, :] - 2.0 * inner) / source_rows.shape[1]


def into_slots(ordering, matrix):
    positions = jnp.arange(matrix.shape[0], dtype=jnp.int32)
    selector = (positions[:, None] == ordering[None, :]).astype(jnp.bfloat16)
    return jnp.dot(selector, matrix, preferred_element_type=jnp.float32).astype(jnp.bfloat16)


def out_of_slots(ordering, matrix):
    positions = jnp.arange(matrix.shape[0], dtype=jnp.int32)
    selector = (ordering[:, None] == positions[None, :]).astype(jnp.bfloat16)
    return jnp.dot(selector, matrix, preferred_element_type=jnp.float32).astype(jnp.bfloat16)


def shards(sources, targets, source_order, target_order):
    rows_dev = sources.shape[0]
    width = sources.shape[1]
    sent_sources = into_slots(source_order, sources)
    sent_targets = into_slots(target_order, targets)
    local_sources, local_targets = (
        lax.all_to_all(sent_sources, "cluster", split_axis=0, concat_axis=0, tiled=True),
        lax.all_to_all(sent_targets, "cluster", split_axis=0, concat_axis=0, tiled=True),
    )
    cluster_targets = lax.all_gather(local_targets, "row", axis=0, tiled=True)
    columns = cluster_targets.shape[0]
    span = 512
    pieces = columns // span
    target_norms = square_sums(cluster_targets)
    target_blocks = cluster_targets.reshape(pieces, span, width)
    norm_blocks = target_norms.reshape(pieces, span)
    source_norms = square_sums(local_sources)
    log_mass = -math.log(columns)

    def row_lse(potential):

        def row_advance(carry, item):
            running, totals = carry
            block, block_norms, block_potential = item
            scores = (
                block_potential[None, :]
                - cost_panel(local_sources, source_norms, block, block_norms)
            ) / entropy_weight
            highest = jnp.maximum(running, jnp.max(scores, axis=1))
            totals = totals * jnp.exp(running - highest) + jnp.sum(
                jnp.exp(scores - highest[:, None]), axis=1
            )
            return ((highest, totals), None)

        start = (jnp.full((rows_dev,), -jnp.inf, jnp.float32), jnp.zeros((rows_dev,), jnp.float32))
        (running, totals), unused = lax.scan(
            row_advance, start, (target_blocks, norm_blocks, potential.reshape(pieces, span))
        )
        return running + jnp.log(totals)

    def column_lse(source_potential):

        def column_advance(carry, item):
            block, block_norms = item
            scores = (
                source_potential[:, None]
                - cost_panel(local_sources, source_norms, block, block_norms)
            ) / entropy_weight
            highest = jnp.max(scores, axis=0)
            return (carry, (highest, jnp.sum(jnp.exp(scores - highest[None, :]), axis=0)))

        unused, (peaks, totals) = lax.scan(column_advance, 0, (target_blocks, norm_blocks))
        peaks = peaks.reshape(-1)
        totals = totals.reshape(-1)
        highest = lax.pmax(peaks, "row")
        summed = lax.psum(totals * jnp.exp(peaks - highest), "row")
        return highest + jnp.log(summed)

    target_potential = jnp.zeros((columns,), jnp.float32)
    for repeat in range(ITERS):
        source_potential = entropy_weight * (log_mass - row_lse(target_potential))
        column_norm = column_lse(source_potential)
        target_potential = entropy_weight * (log_mass - column_norm)
    block = cluster_targets
    block_norms = target_norms
    scores = (
        source_potential[:, None] - cost_panel(local_sources, source_norms, block, block_norms)
    ) / entropy_weight
    weights = jnp.exp(scores - column_norm[None, :]).astype(jnp.bfloat16)
    target_map = lax.psum_scatter(
        jnp.einsum("ij,id->jd", weights, local_sources, preferred_element_type=jnp.float32).astype(
            jnp.bfloat16
        ),
        "row",
        scatter_dimension=0,
        tiled=True,
    )
    row_norm = row_lse(target_potential)

    def accumulate(carry, item):
        block, block_norms, block_potential = item
        scores = (
            block_potential[None, :] - cost_panel(local_sources, source_norms, block, block_norms)
        ) / entropy_weight
        weights = jnp.exp(scores - row_norm[:, None]).astype(jnp.bfloat16)
        return (carry + jnp.dot(weights, block, preferred_element_type=jnp.float32), None)

    source_sums, unused = lax.scan(
        accumulate,
        jnp.zeros((rows_dev, width), jnp.float32),
        (target_blocks, norm_blocks, target_potential.reshape(pieces, span)),
    )
    source_map = source_sums.astype(jnp.bfloat16)
    back_sources, back_targets = (
        lax.all_to_all(source_map, "cluster", split_axis=0, concat_axis=0, tiled=True),
        lax.all_to_all(target_map, "cluster", split_axis=0, concat_axis=0, tiled=True),
    )
    return (out_of_slots(source_order, back_sources), out_of_slots(target_order, back_targets))


def solution(mesh):
    return jax.shard_map(
        shards,
        mesh=mesh,
        in_specs=(
            P(("cluster", "row"), None),
            P(("cluster", "row"), None),
            P(("cluster", "row")),
            P(("cluster", "row")),
        ),
        out_specs=(P(("cluster", "row"), None), P(("cluster", "row"), None)),
        check_vma=False,
    )
```

profile of v0, /device:TPU:1, one launch (start us, length us, event | category | flops | bytes accessed | tf_op | source)
XLA Modules:
  0.0 678.2 jit_solution(1268138748987792291)
XLA Ops:
  9.0 12.2 %all_to_all.48 = bf16[8,32,512]{2,1,0:T(8,128)(2,1)} all-to-all(bf16[8,32,512]{2,1,0:T(8,128)(2,1)S(1)} %bitcast.260), channel_id=1, replica_groups=mesh['cluster'=8,'row'=16] {'cluster'}, dimensions={0} | all-to-all | bytes 524288 | tf_op jit(solution)/shard_map/all_to_all | solution.py:40
  21.2 1.9 convolution_convert_fusion.4
  23.1 4.4 all-to-all-start
  27.6 6.4 all-to-all-done
  34.2 39.4 %all-gather.2.cloned.1.call-done = bf16[4096,512]{1,0:T(8,128)(2,1)} async-done(((bf16[256,512]{1,0:T(8,128)(2,1)}), bf16[4096,512]{1,0:T(8,128)(2,1)}) %all-gather.2.cloned.1.call-update) | async-done | bytes 4194320 | tf_op jit(solution)/shard_map/all_gather | solution.py:42
  73.6 3.1 multiply_reduce_fusion
  76.7 12.7 %while.102 = (s32[]{:T(128)}, f32[256]{0:T(256)S(1)}, f32[256]{0:T(256)S(1)}, f32[256]{0:T(256)S(1)}, f32[8,512]{1,0:T(8,128)S(1)}, /*index=5*/bf16[8,512,512]{2...) while((s32[]{:T(128)}, f32[256]{0:T(256)S(1)}, f32[256]{0:T(256)S(1)}, ...), condition=%wide.region_5.6_spmd.clone, body=%wide.region_2.5_spmd.clone.sunk | while | flops 135398656 | bytes 1856108 | solution.py:68
  89.5 13.7 %while.99 = (s32[]{:T(128)}, f32[8,512]{1,0:T(8,128)S(1)}, f32[8,512]{1,0:T(8,128)S(1)}, f32[256]{0:T(256)S(1)}, f32[256]{0:T(256)S(1)}, /*index=5*/f32[8,512]{1...) while((s32[]{:T(128)}, f32[8,512]{1,0:T(8,128)S(1)}, ...), condition=%wide.region_9.10_spmd, body=%wide.region_6.9_spmd.sunk | while | flops 135396352 | bytes 1858161 | solution.py:84
  89.5 1.4 fusion.151
  91.2 1.4 fusion.151
  92.9 1.4 fusion.151
  94.6 1.4 fusion.151
  96.4 1.4 fusion.151
  98.1 1.4 fusion.151
  99.8 1.4 fusion.151
  101.5 1.4 fusion.151
  103.2 58.3 %pmax.21 = f32[4096]{0:T(1024)S(1)} all-reduce(f32[4096]{0:T(1024)S(1)} %bitcast.268), channel_id=1, replica_groups=mesh['cluster'=8,'row'=16] {'row'}, use_global_device_ids=true, to_apply=%region_10.11 | all-reduce | flops 4096 | bytes 32768 | tf_op jit(solution)/shard_map/pmax | solution.py:87
  161.5 55.6 %psum.21 = f32[4096]{0:T(1024)S(1)} all-reduce(f32[4096]{0:T(1024)S(1)} %exponential_multiply_fusion.2), channel_id=1, replica_groups=mesh['cluster'=8,'row'=16] {'row'}, use_global_device_ids=true, to_apply=%region_11.12 | all-reduce | flops 4096 | bytes 32768 | tf_op jit(solution)/shard_map/psum | solution.py:88
  217.1 12.8 %while.103 = (s32[]{:T(128)}, f32[256]{0:T(256)S(1)}, f32[256]{0:T(256)S(1)}, f32[8,512]{1,0:T(8,128)S(1)}, f32[256]{0:T(256)S(1)}, /*index=5*/f32[8,512]{1,0:T(...) while((s32[]{:T(128)}, f32[256]{0:T(256)S(1)}, ...), condition=%wide.region_15.16_spmd.clone, body=%wide.region_12.15_spmd.clone.sunk | while | flops 135398656 | bytes 1862260 | solution.py:68
  217.2 1.4 fusion.161
  218.8 1.4 fusion.161
  223.6 1.4 fusion.161
  228.4 1.4 fusion.161
  230.0 13.7 %while.100 = (s32[]{:T(128)}, f32[8,512]{1,0:T(8,128)S(1)}, f32[8,512]{1,0:T(8,128)S(1)}, f32[256]{0:T(256)S(1)}, f32[256]{0:T(256)S(1)}, /*index=5*/f32[8,512]{...) while((s32[]{:T(128)}, f32[8,512]{1,0:T(8,128)S(1)}, ...), condition=%wide.region_19.20_spmd, body=%wide.region_16.19_spmd.sunk | while | flops 135396352 | bytes 1858161 | solution.py:84
  230.0 1.4 fusion.153
  231.7 1.4 fusion.153
  233.5 1.4 fusion.153
  235.2 1.4 fusion.153
  236.9 1.4 fusion.153
  238.6 1.4 fusion.153
  240.3 1.4 fusion.153
  242.0 1.4 fusion.153
  243.7 55.6 %pmax.22 = f32[4096]{0:T(1024)S(1)} all-reduce(f32[4096]{0:T(1024)S(1)} %bitcast.270), channel_id=1, replica_groups=mesh['cluster'=8,'row'=16] {'row'}, use_global_device_ids=true, to_apply=%region_20.21 | all-reduce | flops 4096 | bytes 32768 | tf_op jit(solution)/shard_map/pmax | solution.py:87
  299.4 56.0 %psum.22 = f32[4096]{0:T(1024)S(1)} all-reduce(f32[4096]{0:T(1024)S(1)} %exponential_multiply_fusion.1), channel_id=1, replica_groups=mesh['cluster'=8,'row'=16] {'row'}, use_global_device_ids=true, to_apply=%region_21.22 | all-reduce | flops 4096 | bytes 32768 | tf_op jit(solution)/shard_map/psum | solution.py:88
  355.3 12.8 %while.104 = (s32[]{:T(128)}, f32[256]{0:T(256)S(1)}, f32[256]{0:T(256)S(1)}, f32[8,512]{1,0:T(8,128)S(1)}, f32[256]{0:T(256)S(1)}, /*index=5*/f32[8,512]{1,0:T(...) while((s32[]{:T(128)}, f32[256]{0:T(256)S(1)}, ...), condition=%wide.region_25.26_spmd.clone, body=%wide.region_22.25_spmd.clone.sunk | while | flops 135398656 | bytes 1862260 | solution.py:68
  361.8 1.4 fusion.165
  368.2 13.7 %while.101 = (s32[]{:T(128)}, f32[8,512]{1,0:T(8,128)S(1)}, f32[8,512]{1,0:T(8,128)S(1)}, f32[256]{0:T(256)S(1)}, f32[256]{0:T(256)S(1)}, /*index=5*/f32[8,512]{...) while((s32[]{:T(128)}, f32[8,512]{1,0:T(8,128)S(1)}, ...), condition=%wide.region_29.30_spmd, body=%wide.region_26.29_spmd.sunk | while | flops 135396352 | bytes 1858161 | solution.py:84
  368.2 1.4 fusion.155
  369.9 1.4 fusion.155
  371.7 1.4 fusion.155
  373.4 1.4 fusion.155
  375.1 1.4 fusion.155
  376.8 1.4 fusion.155
  378.5 1.4 fusion.155
  380.3 1.4 fusion.155
  382.0 55.6 %pmax.23 = f32[4096]{0:T(1024)S(1)} all-reduce(f32[4096]{0:T(1024)S(1)} %bitcast.272), channel_id=1, replica_groups=mesh['cluster'=8,'row'=16] {'row'}, use_global_device_ids=true, to_apply=%region_30.31 | all-reduce | flops 4096 | bytes 32768 | tf_op jit(solution)/shard_map/pmax | solution.py:87
  437.6 55.6 %psum.23 = f32[4096]{0:T(1024)S(1)} all-reduce(f32[4096]{0:T(1024)S(1)} %exponential_multiply_fusion), channel_id=1, replica_groups=mesh['cluster'=8,'row'=16] {'row'}, use_global_device_ids=true, to_apply=%region_31.32 | all-reduce | flops 4096 | bytes 32768 | tf_op jit(solution)/shard_map/psum | solution.py:88
  493.2 7.0 %convolution_convert_fusion = bf16[4096,512]{1,0:T(8,128)(2,1)} fusion(bf16[256,512]{1,0:T(8,128)(2,1)S(1)} %get-tuple-element.1322, bf16[4096,512]{1,0:T(8,128)(2,1)} %bitcast.254, f32[4096]{0:T(1024)S(1)} %get-tuple-element.614, f32[4096]{0:T(1024)S(1)} %multiply_reduce_fusion, f32[256]{0:T(256)S(1)} %get-tuple-element.1343, f32[256]{0:T(256)S(1)} %get-tuple-element.1345), kind=kOutput, calls=%fused_computation.123 | convolution fusion | flops 2157969408 | bytes 8685568 | tf_op jit(solution)/shard_map/ij,id->jd/dot_general | solution.py:103
  500.2 12.8 %while.105 = (s32[]{:T(128)}, f32[256]{0:T(256)S(1)}, f32[256]{0:T(256)S(1)}, f32[8,512]{1,0:T(8,128)S(1)}, f32[256]{0:T(256)S(1)}, /*index=5*/f32[8,512]{1,0:T(...) while((s32[]{:T(128)}, f32[256]{0:T(256)S(1)}, ...), condition=%wide.region_35.36_spmd.clone, body=%wide.region_32.35_spmd.clone.sunk | while | flops 135398656 | bytes 1862260 | solution.py:68
  503.5 1.4 fusion.169
  508.3 1.4 fusion.169
  513.1 15.4 %while.106 = (s32[]{:T(128)}, f32[256,512]{1,0:T(8,128)S(1)}, f32[8,512]{1,0:T(8,128)S(1)}, f32[256]{0:T(256)S(1)}, f32[8,512]{1,0:T(8,128)S(1)}, /*index=5*/bf1...) while((s32[]{:T(128)}, f32[256,512]{1,0:T(8,128)S(1)}, ...), condition=%wide.region_37.38_spmd.clone, body=%wide.region_36.37_spmd.clone.sunk | while | flops 269746176 | bytes 2374771 | solution.py:120
  513.1 1.9 convolution_add_fusion.2
  515.1 1.9 convolution_add_fusion.2
  517.0 1.9 convolution_add_fusion.2
  518.9 1.9 convolution_add_fusion.2
  520.8 1.9 convolution_add_fusion.2
  522.7 1.9 convolution_add_fusion.2
  524.7 1.9 convolution_add_fusion.2
  526.6 1.9 convolution_add_fusion.2
  528.5 94.9 %all_to_all.49 = bf16[8,32,512]{2,1,0:T(8,128)(2,1)S(1)} all-to-all(bf16[8,32,512]{2,1,0:T(8,128)(2,1)S(1)} %bitcast.255), channel_id=1, replica_groups=mesh['cluster'=8,'row'=16] {'cluster'}, dimensions={0} | all-to-all | bytes 524288 | tf_op jit(solution)/shard_map/all_to_all | solution.py:127
  623.4 33.8 %reduce-scatter.2.cloned.1.call-done = bf16[256,512]{1,0:T(8,128)(2,1)} async-done(((bf16[4096,512]{1,0:T(8,128)(2,1)}), bf16[256,512]{1,0:T(8,128)(2,1)}) %reduce-scatter.2.cloned.1.call-update) | async-done | bytes 262160 | tf_op jit(solution)/shard_map/reduce_scatter | solution.py:102
  657.2 6.7 all-to-all-start.3
  664.9 5.5 all-to-all-done.3
  (340 shorter events, 50.0 us)
Async XLA Ops:
  7.2 1.0 copy-start
  7.2 66.4 %all-gather.2.cloned.1.call-start = ((), (), s32[]{:S(2)}) async-start(), calls=%async_computation.5 | async-start | bytes 4456448 | tf_op jit(solution)/shard_map/all_gather | solution.py:42
  23.1 10.8 %all-to-all-start = ((bf16[8,32,512]{2,1,0:T(8,128)(2,1)}), bf16[8,32,512]{2,1,0:T(8,128)(2,1)S(1)}, u32[]{:S(2)}, u32[]{:S(2)}) async-start(bf16[8,32,512]{2,1,0:T(8,128)(2,1)} %bitcast.15), calls=%async_computation | async-start | bytes 524288 | tf_op jit(solution)/shard_map/all_to_all | solution.py:39
  27.5 629.7 %reduce-scatter.2.cloned.1.call-start = ((), (), s32[]{:S(2)}) async-start(), calls=%async_computation.6 | async-start | bytes 4456448 | tf_op jit(solution)/shard_map/reduce_scatter | solution.py:102
  513.1 150.8 %copy-start.1 = (s32[256]{0:T(256)S(1)}, s32[256]{0:T(256)}, u32[]{:S(2)}) copy-start(s32[256]{0:T(256)} %param.22) | copy-start | bytes 3076
  513.1 157.3 %copy-start.2 = (s32[256]{0:T(256)S(1)}, s32[256]{0:T(256)}, u32[]{:S(2)}) copy-start(s32[256]{0:T(256)} %param.23) | copy-start | bytes 3076
  657.2 13.2 %all-to-all-start.3 = ((bf16[8,32,512]{2,1,0:T(8,128)(2,1)}), bf16[8,32,512]{2,1,0:T(8,128)(2,1)S(1)}, u32[]{:S(2)}, u32[]{:S(2)}) async-start(bf16[8,32,512]{2,1,0:T(8,128)(2,1)} %bitcast.261), calls=%async_computation.4 | async-start | bytes 524288 | tf_op jit(solution)/shard_map/all_to_all | solution.py:128
Sparse Core Ops, SparseCore 0:
  21.3 52.2 all-gather.1
  500.3 156.7 reduce-scatter.1
where the time goes:
time: 682 us; the launch traced here: 678 us
  blocking collectives  444 us (65%)
  matrix products  106 us (16%)
  waiting for transfers between devices  85.2 us (12%)
  between operations  14.3 us (2%)
  starting transfers between devices  11.1 us (2%)
  other arithmetic  10.7 us (2%)
    pmax x3, blocking collectives, column_lse(): highest = lax.pmax(peaks, 'row')  170 us
    psum x3, blocking collectives, column_lse(): summed = lax.psum(totals * jnp.exp(peaks - highest), 'row')  167 us
    all_to_all x1, blocking collectives, shards(): lax.all_to_all(source_map, 'cluster', split_axis=0, concat_axis=0, tiled=...  94.9 us
    dot_general x56, matrix products, cost_panel(): jnp.einsum('id,jd->ij', source_rows, target_rows, preferred_element_type=...  79.3 us
    all_gather x1, waiting for transfers between devices, shards(): cluster_targets = lax.all_gather(local_targets, 'row', axis=0, tiled=True)  39.4 us
    reduce_scatter x1, waiting for transfers between devices, shards(): lax.psum_scatter(jnp.einsum('ij,id->jd', weights, local_sources, preferre...  33.8 us
    dot_general x8, matrix products, accumulate(): jnp.dot(weights, block, preferred_element_type=jnp.float32)  15 us
  transfers between devices with their start and end apart: 4, of which 4 were waited for; matrix products, arithmetic and copies ran while one was open for 5% of the time, Pallas kernels for 0%

commit v1 on v0

--- a/solution.py
+++ b/solution.py
@@ -85,7 +85,7 @@
         peaks = peaks.reshape(-1)
         totals = totals.reshape(-1)
         highest = lax.pmax(peaks, "row")
-        summed = lax.psum(totals * jnp.exp(peaks - highest), "row")
+        summed = jnp.sum(lax.all_gather(totals * jnp.exp(peaks - highest), "row"), axis=0)
         return highest + jnp.log(summed)
 
     target_potential = jnp.zeros((columns,), jnp.float32)

time: 682 us -> 544 us (0.80)
  blocking collectives: 444 us -> 302 us
    psum x3 -> x0, blocking collectives: 167 us -> none  [column_lse(): summed = lax.psum(totals * jnp.exp(peaks - highest), 'row')]
    all_gather x0 -> x3, blocking collectives: none -> 48.4 us  [column_lse(): lax.all_gather(totals * jnp.exp(peaks - highest), 'row')]
    all_to_all x1, blocking collectives: 94.9 us -> 67.9 us  [shards(): lax.all_to_all(source_map, 'cluster', split_axis=0, concat_axis=0, tiled=...]
  transfers between devices with their start and end apart: 4 -> 4, of which waited for: 4 -> 4; matrix products, arithmetic and copies ran while one was open for 5% -> 6% of each run, Pallas kernels for 0% -> 0%
where the time goes in v1:
time: 544 us; the launch traced here: 541 us
  blocking collectives  302 us (56%)
  matrix products  108 us (20%)
  waiting for transfers between devices  86.3 us (16%)
  between operations  14.4 us (3%)
  starting transfers between devices  11.1 us (2%)
  other arithmetic  10.9 us (2%)
    pmax x3, blocking collectives, column_lse(): highest = lax.pmax(peaks, 'row')  174 us
    dot_general x56, matrix products, cost_panel(): jnp.einsum('id,jd->ij', source_rows, target_rows, preferred_element_type=...  79.3 us
    all_to_all x1, blocking collectives, shards(): lax.all_to_all(source_map, 'cluster', split_axis=0, concat_axis=0, tiled=...  67.9 us
    all_gather x3, blocking collectives, column_lse(): lax.all_gather(totals * jnp.exp(peaks - highest), 'row')  48.4 us
    all_gather x1, waiting for transfers between devices, shards(): cluster_targets = lax.all_gather(local_targets, 'row', axis=0, tiled=True)  39.4 us
    reduce_scatter x1, waiting for transfers between devices, shards(): lax.psum_scatter(jnp.einsum('ij,id->jd', weights, local_sources, preferre...  35 us
    dot_general x8, matrix products, accumulate(): jnp.dot(weights, block, preferred_element_type=jnp.float32)  17.3 us
    all_to_all x1, blocking collectives, shards(): lax.all_to_all(sent_targets, 'cluster', split_axis=0, concat_axis=0, tile...  12.2 us
  transfers between devices with their start and end apart: 4, of which 4 were waited for; matrix products, arithmetic and copies ran while one was open for 6% of the time, Pallas kernels for 0%

profile of v1, /device:TPU:1, one launch (start us, length us, event | category | flops | bytes accessed | tf_op | source)
XLA Modules:
  0.0 540.7 jit_solution(14654441921452973470)
XLA Ops:
  9.0 12.2 %all_to_all.48 = bf16[8,32,512]{2,1,0:T(8,128)(2,1)} all-to-all(bf16[8,32,512]{2,1,0:T(8,128)(2,1)S(1)} %bitcast.260), channel_id=1, replica_groups=mesh['cluster'=8,'row'=16] {'cluster'}, dimensions={0} | all-to-all | bytes 524288 | tf_op jit(solution)/shard_map/all_to_all | solution.py:40
  21.2 1.9 convolution_convert_fusion.4
  23.1 4.4 all-to-all-start
  27.6 6.4 %all-to-all-done = bf16[8,32,512]{2,1,0:T(8,128)(2,1)S(1)} async-done(((bf16[8,32,512]{2,1,0:T(8,128)(2,1)}), bf16[8,32,512]{2,1,0:T(8,128)(2,1)S(1)}, u32[]{:S(2)}, u32[]{:S(2)}) %all-to-all-start) | async-done | bytes 262176 | tf_op jit(solution)/shard_map/all_to_all | solution.py:39
  34.2 39.4 %all-gather.5.cloned.1.call-done = bf16[4096,512]{1,0:T(8,128)(2,1)} async-done(((bf16[256,512]{1,0:T(8,128)(2,1)}), bf16[4096,512]{1,0:T(8,128)(2,1)}) %all-gather.5.cloned.1.call-update) | async-done | bytes 4194320 | tf_op jit(solution)/shard_map/all_gather | solution.py:42
  73.6 3.1 multiply_reduce_fusion
  76.7 12.7 %while.102 = (s32[]{:T(128)}, f32[256]{0:T(256)S(1)}, f32[256]{0:T(256)S(1)}, f32[256]{0:T(256)S(1)}, f32[8,512]{1,0:T(8,128)S(1)}, /*index=5*/bf16[8,512,512]{2...) while((s32[]{:T(128)}, f32[256]{0:T(256)S(1)}, f32[256]{0:T(256)S(1)}, ...), condition=%wide.region_5.6_spmd.clone, body=%wide.region_2.5_spmd.clone.sunk | while | flops 135398656 | bytes 1856108 | solution.py:68
  89.5 13.7 %while.99 = (s32[]{:T(128)}, f32[8,512]{1,0:T(8,128)S(1)}, f32[8,512]{1,0:T(8,128)S(1)}, f32[256]{0:T(256)S(1)}, f32[256]{0:T(256)S(1)}, /*index=5*/f32[8,512]{1...) while((s32[]{:T(128)}, f32[8,512]{1,0:T(8,128)S(1)}, ...), condition=%wide.region_9.10_spmd, body=%wide.region_6.9_spmd.sunk | while | flops 135396352 | bytes 1858161 | solution.py:84
  89.5 1.4 fusion.151
  91.2 1.4 fusion.151
  92.9 1.4 fusion.151
  94.6 1.4 fusion.151
  96.4 1.4 fusion.151
  98.1 1.4 fusion.151
  99.8 1.4 fusion.151
  101.5 1.4 fusion.151
  103.2 58.3 %pmax.21 = f32[4096]{0:T(1024)S(1)} all-reduce(f32[4096]{0:T(1024)S(1)} %bitcast.268), channel_id=1, replica_groups=mesh['cluster'=8,'row'=16] {'row'}, use_global_device_ids=true, to_apply=%region_10.11 | all-reduce | flops 4096 | bytes 32768 | tf_op jit(solution)/shard_map/pmax | solution.py:87
  161.5 16.0 %all-gather = f32[65536]{0:T(1024)S(1)} all-gather(f32[4096]{0:T(1024)S(1)} %exponential_multiply_fusion.2), channel_id=2, replica_groups=mesh['cluster'=8,'row'=16] {'row'}, dimensions={0}, use_global_device_ids=true | all-gather | bytes 278528 | tf_op jit(solution)/shard_map/all_gather | solution.py:88
  177.7 12.8 %while.103 = (s32[]{:T(128)}, f32[256]{0:T(256)S(1)}, f32[256]{0:T(256)S(1)}, f32[8,512]{1,0:T(8,128)S(1)}, f32[256]{0:T(256)S(1)}, /*index=5*/f32[8,512]{1,0:T(...) while((s32[]{:T(128)}, f32[256]{0:T(256)S(1)}, ...), condition=%wide.region_15.16_spmd.clone, body=%wide.region_12.15_spmd.clone.sunk | while | flops 135398656 | bytes 1862260 | solution.py:68
  182.5 1.4 fusion.161
  188.9 1.4 fusion.161
  190.5 13.7 %while.100 = (s32[]{:T(128)}, f32[8,512]{1,0:T(8,128)S(1)}, f32[8,512]{1,0:T(8,128)S(1)}, f32[256]{0:T(256)S(1)}, f32[256]{0:T(256)S(1)}, /*index=5*/f32[8,512]{...) while((s32[]{:T(128)}, f32[8,512]{1,0:T(8,128)S(1)}, ...), condition=%wide.region_19.20_spmd, body=%wide.region_16.19_spmd.sunk | while | flops 135396352 | bytes 1858161 | solution.py:84
  190.6 1.4 fusion.153
  192.3 1.4 fusion.153
  194.0 1.4 fusion.153
  195.7 1.4 fusion.153
  197.4 1.4 fusion.153
  199.1 1.4 fusion.153
  200.9 1.4 fusion.153
  202.6 1.4 fusion.153
  204.3 58.1 %pmax.22 = f32[4096]{0:T(1024)S(1)} all-reduce(f32[4096]{0:T(1024)S(1)} %bitcast.270), channel_id=1, replica_groups=mesh['cluster'=8,'row'=16] {'row'}, use_global_device_ids=true, to_apply=%region_20.21 | all-reduce | flops 4096 | bytes 32768 | tf_op jit(solution)/shard_map/pmax | solution.py:87
  262.4 16.6 %all-gather.1 = f32[65536]{0:T(1024)S(1)} all-gather(f32[4096]{0:T(1024)S(1)} %exponential_multiply_fusion.1), channel_id=3, replica_groups=mesh['cluster'=8,'row'=16] {'row'}, dimensions={0}, use_global_device_ids=true | all-gather | bytes 278528 | tf_op jit(solution)/shard_map/all_gather | solution.py:88
  279.2 12.8 %while.104 = (s32[]{:T(128)}, f32[256]{0:T(256)S(1)}, f32[256]{0:T(256)S(1)}, f32[8,512]{1,0:T(8,128)S(1)}, f32[256]{0:T(256)S(1)}, /*index=5*/f32[8,512]{1,0:T(...) while((s32[]{:T(128)}, f32[256]{0:T(256)S(1)}, ...), condition=%wide.region_25.26_spmd.clone, body=%wide.region_22.25_spmd.clone.sunk | while | flops 135398656 | bytes 1862260 | solution.py:68
  279.2 1.4 fusion.165
  285.6 1.4 fusion.165
  292.0 13.7 %while.101 = (s32[]{:T(128)}, f32[8,512]{1,0:T(8,128)S(1)}, f32[8,512]{1,0:T(8,128)S(1)}, f32[256]{0:T(256)S(1)}, f32[256]{0:T(256)S(1)}, /*index=5*/f32[8,512]{...) while((s32[]{:T(128)}, f32[8,512]{1,0:T(8,128)S(1)}, ...), condition=%wide.region_29.30_spmd, body=%wide.region_26.29_spmd.sunk | while | flops 135396352 | bytes 1858161 | solution.py:84
  292.1 1.4 fusion.155
  293.8 1.4 fusion.155
  295.5 1.4 fusion.155
  297.2 1.4 fusion.155
  298.9 1.4 fusion.155
  300.7 1.4 fusion.155
  302.4 1.4 fusion.155
  304.1 1.4 fusion.155
  305.8 57.6 %pmax.23 = f32[4096]{0:T(1024)S(1)} all-reduce(f32[4096]{0:T(1024)S(1)} %bitcast.272), channel_id=1, replica_groups=mesh['cluster'=8,'row'=16] {'row'}, use_global_device_ids=true, to_apply=%region_30.31 | all-reduce | flops 4096 | bytes 32768 | tf_op jit(solution)/shard_map/pmax | solution.py:87
  363.4 15.8 %all-gather.2 = f32[65536]{0:T(1024)S(1)} all-gather(f32[4096]{0:T(1024)S(1)} %exponential_multiply_fusion), channel_id=4, replica_groups=mesh['cluster'=8,'row'=16] {'row'}, dimensions={0}, use_global_device_ids=true | all-gather | bytes 278528 | tf_op jit(solution)/shard_map/all_gather | solution.py:88
  379.3 7.0 %convolution_convert_fusion = bf16[4096,512]{1,0:T(8,128)(2,1)} fusion(bf16[256,512]{1,0:T(8,128)(2,1)S(1)} %get-tuple-element.1322, bf16[4096,512]{1,0:T(8,128)(2,1)} %bitcast.254, f32[4096]{0:T(1024)S(1)} %get-tuple-element.614, f32[4096]{0:T(1024)S(1)} %multiply_reduce_fusion, f32[256]{0:T(256)S(1)} %get-tuple-element.1343, f32[256]{0:T(256)S(1)} %get-tuple-element.1345), kind=kOutput, calls=%fused_computation.123 | convolution fusion | flops 2157969408 | bytes 8685568 | tf_op jit(solution)/shard_map/ij,id->jd/dot_general | solution.py:103
  386.3 12.8 %while.105 = (s32[]{:T(128)}, f32[256]{0:T(256)S(1)}, f32[256]{0:T(256)S(1)}, f32[8,512]{1,0:T(8,128)S(1)}, f32[256]{0:T(256)S(1)}, /*index=5*/f32[8,512]{1,0:T(...) while((s32[]{:T(128)}, f32[256]{0:T(256)S(1)}, ...), condition=%wide.region_35.36_spmd.clone, body=%wide.region_32.35_spmd.clone.sunk | while | flops 135398656 | bytes 1862260 | solution.py:68
  388.0 1.4 fusion.169
  389.6 1.4 fusion.169
  396.0 1.4 fusion.169
  399.2 17.6 %while.106 = (s32[]{:T(128)}, f32[256,512]{1,0:T(8,128)S(1)}, f32[8,512]{1,0:T(8,128)S(1)}, f32[256]{0:T(256)S(1)}, f32[8,512]{1,0:T(8,128)S(1)}, /*index=5*/bf1...) while((s32[]{:T(128)}, f32[256,512]{1,0:T(8,128)S(1)}, ...), condition=%wide.region_37.38_spmd.clone, body=%wide.region_36.37_spmd.clone.sunk | while | flops 269746176 | bytes 2374771 | solution.py:120
  399.2 2.1 convolution_add_fusion.2
  401.4 2.1 convolution_add_fusion.2
  403.6 2.1 convolution_add_fusion.2
  405.8 2.2 convolution_add_fusion.2
  408.0 2.1 convolution_add_fusion.2
  410.2 2.2 convolution_add_fusion.2
  412.5 2.1 convolution_add_fusion.2
  414.7 2.1 convolution_add_fusion.2
  416.9 67.9 %all_to_all.49 = bf16[8,32,512]{2,1,0:T(8,128)(2,1)S(1)} all-to-all(bf16[8,32,512]{2,1,0:T(8,128)(2,1)S(1)} %bitcast.255), channel_id=1, replica_groups=mesh['cluster'=8,'row'=16] {'cluster'}, dimensions={0} | all-to-all | bytes 524288 | tf_op jit(solution)/shard_map/all_to_all | solution.py:127
  484.7 35.0 %reduce-scatter.2.cloned.1.call-done = bf16[256,512]{1,0:T(8,128)(2,1)} async-done(((bf16[4096,512]{1,0:T(8,128)(2,1)}), bf16[256,512]{1,0:T(8,128)(2,1)}) %reduce-scatter.2.cloned.1.call-update) | async-done | bytes 262160 | tf_op jit(solution)/shard_map/reduce_scatter | solution.py:102
  519.7 6.7 %all-to-all-start.3 = ((bf16[8,32,512]{2,1,0:T(8,128)(2,1)}), bf16[8,32,512]{2,1,0:T(8,128)(2,1)S(1)}, u32[]{:S(2)}, u32[]{:S(2)}) async-start(bf16[8,32,512]{2,1,0:T(8,128)(2,1)} %bitcast.261), calls=%async_computation.4 | async-start | bytes 524288 | tf_op jit(solution)/shard_map/all_to_all | solution.py:128
  527.4 5.5 %all-to-all-done.3 = bf16[8,32,512]{2,1,0:T(8,128)(2,1)S(1)} async-done(((bf16[8,32,512]{2,1,0:T(8,128)(2,1)}), bf16[8,32,512]{2,1,0:T(8,128)(2,1)S(1)}, u32[]{:S(2)}, u32[]{:S(2)}) %all-to-all-start.3) | async-done | bytes 262176 | tf_op jit(solution)/shard_map/all_to_all | solution.py:128
  (346 shorter events, 50.3 us)
Async XLA Ops:
  7.2 1.0 copy-start
  7.2 66.4 %all-gather.5.cloned.1.call-start = ((), (), s32[]{:S(2)}) async-start(), calls=%async_computation.5 | async-start | bytes 4456448 | tf_op jit(solution)/shard_map/all_gather | solution.py:42
  23.1 10.8 %all-to-all-start = ((bf16[8,32,512]{2,1,0:T(8,128)(2,1)}), bf16[8,32,512]{2,1,0:T(8,128)(2,1)S(1)}, u32[]{:S(2)}, u32[]{:S(2)}) async-start(bf16[8,32,512]{2,1,0:T(8,128)(2,1)} %bitcast.15), calls=%async_computation | async-start | bytes 524288 | tf_op jit(solution)/shard_map/all_to_all | solution.py:39
  27.5 492.2 %reduce-scatter.2.cloned.1.call-start = ((), (), s32[]{:S(2)}) async-start(), calls=%async_computation.6 | async-start | bytes 4456448 | tf_op jit(solution)/shard_map/reduce_scatter | solution.py:102
  399.2 127.2 %copy-start.1 = (s32[256]{0:T(256)S(1)}, s32[256]{0:T(256)}, u32[]{:S(2)}) copy-start(s32[256]{0:T(256)} %param.22) | copy-start | bytes 3076
  399.2 133.7 %copy-start.2 = (s32[256]{0:T(256)S(1)}, s32[256]{0:T(256)}, u32[]{:S(2)}) copy-start(s32[256]{0:T(256)} %param.23) | copy-start | bytes 3076
  519.7 13.2 %all-to-all-start.3 = ((bf16[8,32,512]{2,1,0:T(8,128)(2,1)}), bf16[8,32,512]{2,1,0:T(8,128)(2,1)S(1)}, u32[]{:S(2)}, u32[]{:S(2)}) async-start(bf16[8,32,512]{2,1,0:T(8,128)(2,1)} %bitcast.261), calls=%async_computation.4 | async-start | bytes 524288 | tf_op jit(solution)/shard_map/all_to_all | solution.py:128
Sparse Core Ops, SparseCore 0:
  21.3 52.2 all-gather.4
  386.4 133.2 reduce-scatter.1
